TPU v7x, 512 devices: a whole 4x8x8 slice. The times are simulated.
512 devices in a mesh: kvh: 8 (over y), qh: 4 (over x_hi, core), req: 16 (over x_lo, z).
Axes of the slice: x: 4 (x_hi: 2, x_lo: 2; x = x_hi * 2 + x_lo), y: 8, z: 8, core: 2. Of those that a mesh axis runs over, the one named last changes fastest.
Arguments:
- queries: bfloat16 [32, 1024, 64, 128], P('req', None, ('kvh', 'qh')), may hold values from -12 to 12
- stretch_keys: bfloat16 [32, 1024, 8, 128], P('req', 'qh', 'kvh'), may hold values from -6 to 6
- stretch_values: bfloat16 [32, 1024, 8, 128], P('req', 'qh', 'kvh'), may hold values from -6 to 6
- cache_keys: bfloat16 [32, 1024, 8, 128], P('req', None, 'kvh'), may hold values from -6 to 6
- cache_values: bfloat16 [32, 1024, 8, 128], P('req', None, 'kvh'), may hold values from -6 to 6
- slot_of_req: int32 [32], replicated, may hold values from 0 to 31, each once
- cache_len: int32 [32], P('req'), may hold values from 128 to 1024, as said below
Outputs:
- attended: bfloat16 [32, 1024, 64, 128], P('req', None, ('kvh', 'qh'))
Inputs may be any that keep to these rules, and one draw needn't show every extreme that they name: `cache_len`: one request in every draw has exactly 1024 cached positions.
All inputs are finite; a program needn't handle non-finite values.
Results may differ from a plain program's by a relative error of at most 0.0035.
Values may be sent and summed in bfloat16 or wider, within the bound.
A program may use at most 64 MiB of HBM per device.

v0:
```python
import jax
import jax.numpy as jnp
from jax import lax
from jax.sharding import PartitionSpec as P

H = 64
KVH = 8


def relocate(keys, values, slot_of_req, req_count):
    slots, span, kv_heads, head_dim = keys.shape
    piece = span // req_count
    split_keys = keys.reshape(slots, req_count, piece, kv_heads, head_dim)
    split_values = values.reshape(slots, req_count, piece, kv_heads, head_dim)
    spread_keys, spread_values = (
        lax.all_to_all(split_keys, "req", split_axis=1, concat_axis=0, tiled=True),
        lax.all_to_all(split_values, "req", split_axis=1, concat_axis=0, tiled=True),
    )
    picked_keys = jnp.take(spread_keys, slot_of_req, axis=0)
    picked_values = jnp.take(spread_values, slot_of_req, axis=0)
    got_keys, got_values = (
        lax.all_to_all(picked_keys, "req", split_axis=0, concat_axis=1, tiled=True),
        lax.all_to_all(picked_values, "req", split_axis=0, concat_axis=1, tiled=True),
    )
    return (
        got_keys.reshape(slots, span, kv_heads, head_dim),
        got_values.reshape(slots, span, kv_heads, head_dim),
    )


def on_device(
    queries, stretch_keys, stretch_values, cache_keys, cache_values, slot_of_req, cache_len
):
    req_count = lax.axis_size("req")
    local_reqs, stretch, head_count, head_dim = queries.shape
    group = H // KVH
    kv_local = lax.axis_index("qh") * head_count // group
    new_keys, new_values = (
        lax.all_gather(stretch_keys, "qh", axis=1, tiled=True),
        lax.all_gather(stretch_values, "qh", axis=1, tiled=True),
    )
    own_keys, own_values = relocate(cache_keys, cache_values, slot_of_req, req_count)
    keys_c = lax.dynamic_index_in_dim(own_keys, kv_local, 2, keepdims=False)
    values_c = lax.dynamic_index_in_dim(own_values, kv_local, 2, keepdims=False)
    keys_n = lax.dynamic_index_in_dim(new_keys, kv_local, 2, keepdims=False)
    values_n = lax.dynamic_index_in_dim(new_values, kv_local, 2, keepdims=False)
    span = keys_c.shape[1]
    rows = min(512, stretch)
    blocks = stretch // rows
    factor = head_dim ** (-0.5)

    def one_block(index):
        request = index // (head_count * blocks)
        head = index // blocks % head_count
        first = index % blocks * rows
        query = lax.dynamic_slice(
            queries, (request, first, head, 0), (1, rows, 1, head_dim)
        ).reshape(rows, head_dim)
        key_c = lax.dynamic_index_in_dim(keys_c, request, 0, keepdims=False)
        value_c = lax.dynamic_index_in_dim(values_c, request, 0, keepdims=False)
        key_n = lax.dynamic_index_in_dim(keys_n, request, 0, keepdims=False)
        value_n = lax.dynamic_index_in_dim(values_n, request, 0, keepdims=False)
        length = lax.dynamic_index_in_dim(cache_len, request, 0, keepdims=False)
        score_c = jnp.einsum("qd,kd->qk", query, key_c, preferred_element_type=jnp.float32) * factor
        score_n = jnp.einsum("qd,kd->qk", query, key_n, preferred_element_type=jnp.float32) * factor
        seen_c = (jnp.arange(span, dtype=jnp.int32) < length)[None, :]
        seen_n = (
            jnp.arange(stretch, dtype=jnp.int32)[None, :]
            <= (first + jnp.arange(rows, dtype=jnp.int32))[:, None]
        )
        top_c = jnp.max(jnp.where(seen_c, score_c, -jnp.inf), axis=1)
        top_n = jnp.max(jnp.where(seen_n, score_n, -jnp.inf), axis=1)
        top = jnp.maximum(top_c, top_n)[:, None]
        weight_c = jnp.where(seen_c, jnp.exp(score_c - top), 0.0)
        weight_n = jnp.where(seen_n, jnp.exp(score_n - top), 0.0)
        total = jnp.sum(weight_c, axis=1) + jnp.sum(weight_n, axis=1)
        mixed = jnp.dot(weight_c.astype(jnp.bfloat16), value_c, preferred_element_type=jnp.float32)
        mixed = mixed + jnp.dot(
            weight_n.astype(jnp.bfloat16), value_n, preferred_element_type=jnp.float32
        )
        return (mixed / total[:, None]).astype(jnp.bfloat16)

    count = local_reqs * head_count * blocks
    results = lax.map(one_block, jnp.arange(count, dtype=jnp.int32))
    results = results.reshape(local_reqs, head_count, blocks, rows, head_dim)
    return jnp.transpose(results, (0, 2, 3, 1, 4)).reshape(
        local_reqs, stretch, head_count, head_dim
    )


def solution(mesh):
    return jax.shard_map(
        on_device,
        mesh=mesh,
        in_specs=(
            P("req", None, ("kvh", "qh"), None),
            P("req", "qh", "kvh", None),
            P("req", "qh", "kvh", None),
            P("req", None, "kvh", None),
            P("req", None, "kvh", None),
            P(),
            P("req"),
        ),
        out_specs=P("req", None, ("kvh", "qh"), None),
        check_vma=False,
    )
```

profile of v0, /device:TPU:1, one launch (start us, length us, event | category | flops | bytes accessed | tf_op | source)
XLA Modules:
  0.0 172.7 jit_solution(8115835762924543527)
XLA Ops:
  0.0 1.9 %copy.23 = bf16[2,16,64,1,128]{4,2,0,3,1:T(8,128)(2,1)} copy(bf16[2,16,64,1,128]{4,2,1,0,3:T(8,128)(2,1)} %bitcast.101) | data formatting | bytes 1048576 | tf_op jit(solution)/shard_map/reshape | solution.py:13
  1.9 11.9 %all-to-all-start = ((bf16[2,16,64,1,128]{4,2,0,3,1:T(8,128)(2,1)}), bf16[2,16,64,1,128]{4,2,0,3,1:T(8,128)(2,1)S(1)}, u32[]{:S(2)}, u32[]{:S(2)}) async-start(bf16[2,16,64,1,128]{4,2,0,3,1:T(8,128)(2,1)} %copy.23), calls=%async_computation | async-start | bytes 1048576 | tf_op jit(solution)/shard_map/all_to_all | solution.py:16
  13.8 0.8 copy.27
  14.7 12.9 %all-to-all-done = bf16[2,16,64,1,128]{4,2,0,3,1:T(8,128)(2,1)S(1)} async-done(((bf16[2,16,64,1,128]{4,2,0,3,1:T(8,128)(2,1)}), bf16[2,16,64,1,128]{4,2,0,3,1:T(8,128)(2,1)S(1)}, u32[]{:S(2)}, u32[]{:S(2)}) %all-to-all-start) | async-done | bytes 524320 | tf_op jit(solution)/shard_map/all_to_all | solution.py:16
  27.6 6.0 %all-to-all-start.2 = ((bf16[2,16,64,1,128]{4,2,0,3,1:T(8,128)(2,1)}), bf16[2,16,64,1,128]{4,2,0,3,1:T(8,128)(2,1)S(1)}, u32[]{:S(2)}, u32[]{:S(2)}) async-start(bf16[2,16,64,1,128]{4,2,0,3,1:T(8,128)(2,1)} %copy.27), calls=%async_computation.2 | async-start | bytes 1048576 | tf_op jit(solution)/shard_map/all_to_all | solution.py:17
  34.3 12.2 %all-to-all-done.2 = bf16[2,16,64,1,128]{4,2,0,3,1:T(8,128)(2,1)S(1)} async-done(((bf16[2,16,64,1,128]{4,2,0,3,1:T(8,128)(2,1)}), bf16[2,16,64,1,128]{4,2,0,3,1:T(8,128)(2,1)S(1)}, u32[]{:S(2)}, u32[]{:S(2)}) %all-to-all-start.2) | async-done | bytes 524320 | tf_op jit(solution)/shard_map/all_to_all | solution.py:17
  47.2 1.0 fusion.37
  48.1 18.8 %all_to_all.66 = bf16[32,1,64,1,128]{4,2,3,1,0:T(8,128)(2,1)S(1)} all-to-all(bf16[32,1,64,1,128]{4,2,3,1,0:T(8,128)(2,1)S(1)} %get-tuple-element.208), channel_id=1, replica_groups=mesh['kvh'=8,'qh'=4,'req'=16] {'req'}, dimensions={0} | all-to-all | bytes 1048576 | tf_op jit(solution)/shard_map/all_to_all | solution.py:22
  66.9 6.4 %all-to-all-start.3 = ((bf16[32,1,64,1,128]{4,2,3,1,0:T(8,128)(2,1)}), bf16[32,1,64,1,128]{4,2,3,1,0:T(8,128)(2,1)S(1)}, u32[]{:S(2)}, u32[]{:S(2)}) async-start(bf16[32,1,64,1,128]{4,2,3,1,0:T(8,128)(2,1)} %get-tuple-element.207), calls=%async_computation.3 | async-start | bytes 1048576 | tf_op jit(solution)/shard_map/all_to_all | solution.py:23
  73.3 1.4 copy.31
  74.7 12.7 %all_gather.6 = bf16[2,1024,1,128]{3,1,0,2:T(8,128)(2,1)S(1)} all-gather(bf16[2,256,1,128]{3,1,0,2:T(8,128)(2,1)S(1)} %bitcast.104), channel_id=1, replica_groups=mesh['kvh'=8,'qh'=4,'req'=16] {'qh'}, dimensions={1}, use_global_device_ids=true | all-gather | bytes 655360 | tf_op jit(solution)/shard_map/all_gather | solution.py:39
  87.4 9.2 %all_gather.7 = bf16[2,1024,1,128]{3,1,0,2:T(8,128)(2,1)} all-gather(bf16[2,256,1,128]{3,1,0,2:T(8,128)(2,1)S(1)} %bitcast.105), channel_id=1, replica_groups=mesh['kvh'=8,'qh'=4,'req'=16] {'qh'}, dimensions={1}, use_global_device_ids=true | all-gather | bytes 655360 | tf_op jit(solution)/shard_map/all_gather | solution.py:40
  96.7 72.7 %while.13 = (s32[]{:T(128)}, bf16[8,512,128]{2,1,0:T(8,128)(2,1)}, s32[8]{0:T(128)S(1)}, s32[2]{0:T(128)S(1)}, bf16[2,1024,2,128]{3,1,2,0:T(8,128)(2,1)S(1)}, /*...) while((s32[]{:T(128)}, bf16[8,512,128]{2,1,0:T(8,128)(2,1)}, ...), condition=%wide.region_5.7_spmd, body=%wide.region_0.6_spmd.sunk | while | flops 550175296 | bytes 16692442 | solution.py:84
  101.2 0.6 iota_compare_fusion.3
  102.4 1.1 fusion.51
  104.5 1.3 fusion.52
  111.5 1.1 fusion.51
  113.6 1.3 fusion.52
  120.5 1.1 fusion.51
  122.7 1.3 fusion.52
  129.6 1.1 fusion.51
  131.8 1.3 fusion.52
  138.7 1.1 fusion.51
  140.9 1.3 fusion.52
  146.6 0.6 iota_compare_fusion.3
  147.8 1.1 fusion.51
  150.0 1.3 fusion.52
  156.9 1.1 fusion.51
  159.1 1.3 fusion.52
  166.0 1.1 fusion.51
  168.1 1.3 fusion.52
  169.5 3.3 %copy.32 = bf16[2,2,2,512,128]{4,1,3,2,0:T(2,128)(2,1)} copy(bf16[2,2,2,512,128]{4,3,2,1,0:T(8,128)(2,1)} %bitcast.98) | data formatting | bytes 2097152 | tf_op jit(solution)/shard_map/reshape | solution.py:85
  (106 shorter events, 31.9 us)
Async XLA Ops:
  0.0 13.8 %copy-start.1 = (bf16[2,1024,1,128]{3,1,2,0:T(8,128)(2,1)S(1)}, bf16[2,1024,1,128]{3,1,2,0:T(8,128)(2,1)}, u32[]{:S(2)}) copy-start(bf16[2,1024,1,128]{3,1,2,0:T(8,128)(2,1)} %param.15) | copy-start | bytes 1572868
  0.0 33.6 %copy-start.4 = (s32[32]{0:T(128)S(1)}, s32[32]{0:T(128)}, u32[]{:S(2)}) copy-start(s32[32]{0:T(128)} %param.16) | copy-start | bytes 388
  1.9 25.6 %all-to-all-start = ((bf16[2,16,64,1,128]{4,2,0,3,1:T(8,128)(2,1)}), bf16[2,16,64,1,128]{4,2,0,3,1:T(8,128)(2,1)S(1)}, u32[]{:S(2)}, u32[]{:S(2)}) async-start(bf16[2,16,64,1,128]{4,2,0,3,1:T(8,128)(2,1)} %copy.23), calls=%async_computation | async-start | bytes 1048576 | tf_op jit(solution)/shard_map/all_to_all | solution.py:16
  27.6 18.9 %all-to-all-start.2 = ((bf16[2,16,64,1,128]{4,2,0,3,1:T(8,128)(2,1)}), bf16[2,16,64,1,128]{4,2,0,3,1:T(8,128)(2,1)S(1)}, u32[]{:S(2)}, u32[]{:S(2)}) async-start(bf16[2,16,64,1,128]{4,2,0,3,1:T(8,128)(2,1)} %copy.27), calls=%async_computation.2 | async-start | bytes 1048576 | tf_op jit(solution)/shard_map/all_to_all | solution.py:17
  48.1 26.6 %copy-start.2 = (bf16[2,256,1,128]{3,1,2,0:T(8,128)(2,1)S(1)}, bf16[2,256,1,128]{3,1,2,0:T(8,128)(2,1)}, u32[]{:S(2)}) copy-start(bf16[2,256,1,128]{3,1,2,0:T(8,128)(2,1)} %param.12) | copy-start | bytes 393220
  66.9 20.5 %copy-start.3 = (bf16[2,256,1,128]{3,1,2,0:T(8,128)(2,1)S(1)}, bf16[2,256,1,128]{3,1,2,0:T(8,128)(2,1)}, u32[]{:S(2)}) copy-start(bf16[2,256,1,128]{3,1,2,0:T(8,128)(2,1)} %param.13) | copy-start | bytes 393220
  66.9 29.8 %all-to-all-start.3 = ((bf16[32,1,64,1,128]{4,2,3,1,0:T(8,128)(2,1)}), bf16[32,1,64,1,128]{4,2,3,1,0:T(8,128)(2,1)S(1)}, u32[]{:S(2)}, u32[]{:S(2)}) async-start(bf16[32,1,64,1,128]{4,2,3,1,0:T(8,128)(2,1)} %get-tuple-element.207), calls=%async_computation.3 | async-start | bytes 1048576 | tf_op jit(solution)/shard_map/all_to_all | solution.py:23
  74.7 22.1 %copy-start.5 = (s32[2]{0:T(128)S(1)}, s32[2]{0:T(128)}, u32[]{:S(2)}) copy-start(s32[2]{0:T(128)} %param.17) | copy-start | bytes 28
  103.5 1.0 copy-start
  112.6 1.0 copy-start
  121.6 1.0 copy-start
  130.7 1.0 copy-start
  139.8 1.0 copy-start
  148.9 1.0 copy-start
  158.0 1.0 copy-start
  167.1 1.0 copy-start
where the time goes:
time: 174 us; the launch traced here: 173 us
  blocking collectives  40.7 us (23%)
  waiting for transfers between devices  25.1 us (14%)
  starting transfers between devices  24.3 us (14%)
  matrix products  23.7 us (14%)
  local copies, waits for them, and re-layouts  22 us (13%)
  loops' own time  21.7 us (12%)
  other arithmetic  15.1 us (9%)
    another operation x1, loops' own time, on_device(): results = lax.map(one_block, jnp.arange(count, dtype=jnp.int32))  21.7 us
    all_to_all x1, blocking collectives, relocate(): lax.all_to_all(picked_keys, 'req', split_axis=0, concat_axis=1, tiled=True)  18.8 us
    all_to_all x1, waiting for transfers between devices, relocate(): lax.all_to_all(split_keys, 'req', split_axis=1, concat_axis=0, tiled=True)  12.9 us
    all_gather x1, blocking collectives, on_device(): lax.all_gather(stretch_keys, 'qh', axis=1, tiled=True)  12.7 us
    all_to_all x1, waiting for transfers between devices, relocate(): lax.all_to_all(split_values, 'req', split_axis=1, concat_axis=0, tiled=True)  12.2 us
    all_to_all x1, starting transfers between devices, relocate(): lax.all_to_all(split_keys, 'req', split_axis=1, concat_axis=0, tiled=True)  11.9 us
    dot_general x8, matrix products, one_block(): jnp.dot(weight_n.astype(jnp.bfloat16), value_n, preferred_element_type=jn...  10.5 us
    all_gather x1, blocking collectives, on_device(): lax.all_gather(stretch_values, 'qh', axis=1, tiled=True)  9.24 us
  transfers between devices with their start and end apart: 3, of which 2 were waited for; matrix products, arithmetic and copies ran while one was open for 2% of the time, Pallas kernels for 0%

commit v1 on v0

v1 whole, which is shorter than its diff:
```python
import functools
import math

import jax
import jax.numpy as jnp
from jax import lax
from jax.experimental import pallas as pl
from jax.experimental.pallas import tpu as pltpu
from jax.sharding import PartitionSpec as P

MESH = pl.DeviceIdType.MESH
HIDDEN = -1e30


def move_kernel(
    n, slot_ref, sk_ref, sv_ref, ck_ref, cv_ref, skb, svb, kcb, vcb,
    spread, picked, local_sem, s_send, s_recv, p1_send, p1_recv, p2_send, p2_recv,
    x_send, x_recv, y_send, y_recv,
):
    me = lax.axis_index("req")
    q = lax.axis_index("qh")
    core = lax.rem(q, 2)
    side = q // 2
    mate = q + 1 - 2 * core
    over = lax.rem(q + 2, 4)
    per = sk_ref.shape[1]
    span = ck_ref.shape[1]
    half = span // 2
    piece = half // n

    barrier = pltpu.get_barrier_semaphore()

    def greet(d, _):
        pl.semaphore_signal(barrier, inc=1, device_id={"req": lax.rem(me + d, n)}, device_id_type=MESH)
        return 0

    lax.fori_loop(1, n, greet, 0)
    for peer in (mate, over):
        pl.semaphore_signal(barrier, inc=1, device_id={"qh": peer}, device_id_type=MESH)

    def rows_of(index, of_side):
        return pl.ds(pl.multiple_of(of_side * half + index * piece, piece), piece)

    own = pl.ds(pl.multiple_of(q * per, per), per)
    own_copies = [
        pltpu.make_async_copy(sk_ref, skb.at[:, own], local_sem.at[0]),
        pltpu.make_async_copy(sv_ref, svb.at[:, own], local_sem.at[1]),
    ]
    for copy in own_copies:
        copy.start()
    mine = pl.ds(2 * me, 2)
    for c, src in enumerate((ck_ref, cv_ref)):
        @pl.when(core == c)
        def _(src=src):
            pltpu.make_async_copy(src.at[:, rows_of(me, side)], spread.at[mine], local_sem.at[2]).start()

    pl.semaphore_wait(barrier, n + 1)

    for c, src in enumerate((ck_ref, cv_ref)):
        @pl.when(core == c)
        def _(src=src):
            def send(d, _):
                to = lax.rem(me + d, n)
                pltpu.make_async_remote_copy(
                    src.at[:, rows_of(to, side)], spread.at[mine], p1_send, p1_recv,
                    device_id={"req": to}, device_id_type=MESH,
                ).start()
                return 0

            lax.fori_loop(1, n, send, 0)

    def stretch(k, peer):
        return [
            pltpu.make_async_remote_copy(
                src, dst.at[:, own], s_send.at[k, i], s_recv.at[k, i],
                device_id={"qh": peer}, device_id_type=MESH,
            )
            for i, (src, dst) in enumerate(((sk_ref, skb), (sv_ref, svb)))
        ]

    to_over = stretch(0, over)
    to_mate = stretch(1, mate)
    for copy in to_over + to_mate:
        copy.start()

    pltpu.make_async_copy(spread.at[mine], spread.at[mine], local_sem.at[2]).wait()
    most = pl.ds(0, 2 * (n - 1))
    pltpu.make_async_copy(spread.at[most], spread.at[most], p1_recv).wait()
    for r in range(2 * n):
        picked[r] = spread[slot_ref[r]]

    for j in range(2):
        for c, dst in enumerate((kcb, vcb)):
            @pl.when(core == c)
            def _(j=j, dst=dst):
                def send(d, _):
                    to = lax.rem(me + d, n)
                    pltpu.make_async_remote_copy(
                        picked.at[2 * to + j], dst.at[j, rows_of(me, side)], p2_send, p2_recv.at[j, d],
                        device_id={"req": to}, device_id_type=MESH,
                    ).start()
                    return 0

                pltpu.make_async_copy(
                    picked.at[2 * me + j], dst.at[j, rows_of(me, side)], p2_recv.at[j, 0]
                ).start()
                lax.fori_loop(1, n, send, 0)

    theirs = pl.ds(pl.multiple_of(over * per, per), per)
    for copy in to_over:
        copy.wait_recv()
    passed = [
        pltpu.make_async_remote_copy(
            dst.at[:, theirs], dst.at[:, theirs], s_send.at[2, i], s_recv.at[2, i],
            device_id={"qh": mate}, device_id_type=MESH,
        )
        for i, dst in enumerate((skb, svb))
    ]
    for copy in passed:
        copy.start()

    def forward(dst, j, d):
        rows = rows_of(lax.rem(me + n - d, n), side)
        pltpu.make_async_copy(picked.at[0], dst.at[j, rows], p2_recv.at[j, d]).wait()
        pltpu.make_async_remote_copy(
            dst.at[j, rows], dst.at[j, rows], x_send, x_recv.at[j, d],
            device_id={"qh": over}, device_id_type=MESH,
        ).start()
        pltpu.make_async_remote_copy(
            dst.at[j, rows], dst.at[j, rows], y_send, y_recv,
            device_id={"qh": mate}, device_id_type=MESH,
        ).start()

    def onward(dst, j, d):
        rows = rows_of(lax.rem(me + n - d, n), 1 - side)
        pltpu.make_async_copy(picked.at[0], dst.at[j, rows], x_recv.at[j, d]).wait()
        pltpu.make_async_remote_copy(
            dst.at[j, rows], dst.at[j, rows], y_send, y_recv,
            device_id={"qh": mate}, device_id_type=MESH,
        ).start()

    for step in (forward, onward):
        for c, dst in enumerate((kcb, vcb)):
            @pl.when(core == c)
            def _(step=step, dst=dst):
                for j in range(2):
                    def body(d, _, j=j):
                        step(dst, j, d)
                        return 0

                    lax.fori_loop(0, n, body, 0)

    pltpu.make_async_copy(kcb, vcb, y_recv).wait()
    for copy in own_copies:
        copy.wait()
    for copy in to_mate:
        copy.wait()
    for copy in to_over:
        copy.wait_send()
    for copy in passed:
        copy.wait()
    pltpu.make_async_copy(spread.at[most], spread.at[most], p1_send).wait()
    pltpu.make_async_copy(spread.at[most], spread.at[most], p2_send).wait()
    pltpu.make_async_copy(spread, spread, x_send).wait()
    pltpu.make_async_copy(kcb, kcb, y_send).wait()


def move(slot_of_req, stretch_keys, stretch_values, cache_keys, cache_values, n):
    reqs, span, dim = cache_keys.shape
    full = jax.ShapeDtypeStruct((reqs, span, dim), cache_keys.dtype)
    piece = span // 2 // n
    any_spec = pl.BlockSpec(memory_space=pl.ANY)
    vmem = pl.BlockSpec(memory_space=pltpu.VMEM)
    dma = pltpu.SemaphoreType.DMA
    return pl.pallas_call(
        functools.partial(move_kernel, n),
        out_shape=(full,) * 4,
        in_specs=[pl.BlockSpec(memory_space=pltpu.SMEM)] + [any_spec] * 4,
        out_specs=(vmem,) * 4,
        scratch_shapes=[
            pltpu.VMEM((2 * n, piece, dim), cache_keys.dtype),
            pltpu.VMEM((2 * n, piece, dim), cache_keys.dtype),
            dma((3,)), dma((3, 2)), dma((3, 2)), dma, dma, dma, dma((2, n)),
            dma, dma((2, n)), dma, dma,
        ],
        compiler_params=pltpu.CompilerParams(collective_id=0, has_side_effects=True),
    )(slot_of_req, stretch_keys, stretch_values, cache_keys, cache_values)


def attend_kernel(len_ref, q_ref, skb, svb, kcb, vcb, o_ref):
    tile, dim = q_ref.shape[1:]
    span = kcb.shape[1]
    tokens = tile // 2
    r = pl.program_id(0)
    i = pl.program_id(1)
    scale = math.log2(math.e) / math.sqrt(dim)
    query = q_ref[0]
    ones = jnp.ones((tokens, dim), jnp.bfloat16)

    def block(carry, keys, values, seen):
        top, acc = carry
        scores = lax.dot_general(query, keys, (((1,), (1,)), ((), ())), preferred_element_type=jnp.float32)
        if seen is not None:
            scores = jnp.where(seen, scores, HIDDEN)
        new = jnp.maximum(top, jnp.max(scores, axis=1, keepdims=True))
        weights = jnp.exp2((scores - new) * scale).astype(jnp.bfloat16)
        wide = jnp.concatenate([values, ones], axis=1)
        acc = acc * jnp.exp2((top - new) * scale) + jnp.dot(weights, wide, preferred_element_type=jnp.float32)
        return new, acc

    def keys_at(ref, b):
        return ref[0, pl.ds(pl.multiple_of(b * tokens, tokens), tokens), :]

    row = lax.broadcasted_iota(jnp.int32, (tile, tokens), 0) // 2
    col = lax.broadcasted_iota(jnp.int32, (tile, tokens), 1)
    carry = (jnp.full((tile, 1), HIDDEN, jnp.float32), jnp.zeros((tile, 2 * dim), jnp.float32))
    carry = block(carry, keys_at(skb, i), keys_at(svb, i), col <= row)
    carry = lax.fori_loop(0, i, lambda b, c: block(c, keys_at(skb, b), keys_at(svb, b), None), carry)
    length = len_ref[r]
    whole = length // tokens
    carry = lax.fori_loop(0, whole, lambda b, c: block(c, keys_at(kcb, b), keys_at(vcb, b), None), carry)
    carry = lax.fori_loop(
        whole, pl.cdiv(length, tokens),
        lambda b, c: block(c, keys_at(kcb, b), keys_at(vcb, b), col < length - b * tokens), carry,
    )
    acc = carry[1]
    o_ref[0] = (acc[:, :dim] / acc[:, dim:]).astype(o_ref.dtype)


def attend(cache_len, queries, skb, svb, kcb, vcb):
    reqs, rows, dim = queries.shape
    tile = 512
    whole = pl.BlockSpec((1,) + skb.shape[1:], lambda r, i, *_: (r, 0, 0))
    tiled = pl.BlockSpec((1, tile, dim), lambda r, i, *_: (r, i, 0))
    return pl.pallas_call(
        attend_kernel,
        out_shape=jax.ShapeDtypeStruct(queries.shape, queries.dtype),
        grid_spec=pltpu.PrefetchScalarGridSpec(
            num_scalar_prefetch=1,
            grid=(reqs, rows // tile),
            in_specs=[tiled, whole, whole, whole, whole],
            out_specs=tiled,
        ),
        compiler_params=pltpu.CompilerParams(dimension_semantics=("arbitrary", "arbitrary")),
    )(cache_len, queries, skb, svb, kcb, vcb)


def on_device(queries, stretch_keys, stretch_values, cache_keys, cache_values, slot_of_req, cache_len):
    reqs, stretch, heads, dim = queries.shape
    flat = [a.reshape(a.shape[0], a.shape[1], dim) for a in (stretch_keys, stretch_values, cache_keys, cache_values)]
    moved = move(slot_of_req, *flat, lax.axis_size("req"))
    out = attend(cache_len, queries.reshape(reqs, stretch * heads, dim), *moved)
    return out.reshape(queries.shape)


def solution(mesh):
    return jax.shard_map(
        on_device,
        mesh=mesh,
        in_specs=(
            P("req", None, ("kvh", "qh"), None),
            P("req", "qh", "kvh", None),
            P("req", "qh", "kvh", None),
            P("req", None, "kvh", None),
            P("req", None, "kvh", None),
            P(),
            P("req"),
        ),
        out_specs=P("req", None, ("kvh", "qh"), None),
        check_vma=False,
    )
```

time: 174 us -> 71.3 us (0.41)
  Pallas kernels: 0 us -> 71.2 us
  blocking collectives: 40.7 us -> 0 us
  waiting for transfers between devices: 25.1 us -> 0 us
  starting transfers between devices: 24.3 us -> 0 us
  matrix products: 23.7 us -> 0 us
  local copies, waits for them, and re-layouts: 22 us -> 0 us
  loops' own time: 21.7 us -> 0 us
  other arithmetic: 15.1 us -> 0 us
    pallas_call x0 -> x2, Pallas kernels: none -> 71.2 us  [the longest x1 38.5 us: move(): pl.pallas_call(functools.partial(move_kernel, n), out_shape=(full,) * 4,...]
    all_to_all x3 -> x0, waiting for transfers between devices: 25.1 us -> none  [the longest x1 12.9 us: relocate(): lax.all_to_all(split_keys, 'req', split_axis=1, concat_axis=0, tiled=True)]
    all_to_all x3 -> x0, starting transfers between devices: 24.3 us -> none  [the longest x1 11.9 us: relocate(): lax.all_to_all(split_keys, 'req', split_axis=1, concat_axis=0, tiled=True)]
    dot_general x32 -> x0, matrix products: 23.7 us -> none  [the longest x8 10.5 us: one_block(): jnp.dot(weight_n.astype(jnp.bfloat16), value_n, preferred_element_type=jn...]
    all_gather x2 -> x0, blocking collectives: 21.9 us -> none  [the longest x1 12.7 us: on_device(): lax.all_gather(stretch_keys, 'qh', axis=1, tiled=True)]
    another operation x1 -> x0, loops' own time: 21.7 us -> none  [on_device(): results = lax.map(one_block, jnp.arange(count, dtype=jnp.int32))]
    all_to_all x1 -> x0, blocking collectives: 18.8 us -> none  [relocate(): lax.all_to_all(picked_keys, 'req', split_axis=0, concat_axis=1, tiled=True)]
    dynamic_slice x16 -> x0, local copies, waits for them, and re-layouts: 9.37 us -> none  [the longest x8 4.71 us: one_block(): length = lax.dynamic_index_in_dim(cache_len, request, 0, keepdims=False)]
  transfers between devices with their start and end apart: 3 -> 0, of which waited for: 2 -> 0; matrix products, arithmetic and copies ran while one was open for 2% -> 0% of each run, Pallas kernels for 0% -> 0%
where the time goes in v1:
time: 71.3 us; the launch traced here: 71.2 us
  Pallas kernels  71.2 us (100%)
    pallas_call x1, Pallas kernels, move(): pl.pallas_call(functools.partial(move_kernel, n), out_shape=(full,) * 4,...  38.5 us
    pallas_call x1, Pallas kernels, attend(): pl.pallas_call(attend_kernel, out_shape=jax.ShapeDtypeStruct(queries.shap...  32.7 us

profile of v1, /device:TPU:1, one launch (start us, length us, event | category | flops | bytes accessed | tf_op | source)
XLA Modules:
  0.0 71.2 jit_solution(729439025849626157)
XLA Ops:
  0.0 38.5 %shard_map.73 = (bf16[2,1024,128]{2,1,0:T(8,128)(2,1)}, bf16[2,1024,128]{2,1,0:T(8,128)(2,1)}, bf16[2,1024,128]{2,1,0:T(8,128)(2,1)}, bf16[2,1024,128]{2,1,0:T(8,128)(2,1)}) custom-call(s32[32]{0:T(128)} %slot_ref.1, bf16[2,256,128]{2,1,0:T(8,128)(2,1)} %bitcast.9, bf16[2,256,128]{2,1,0:T(8,128)(2,1)} %bitcast.10, bf16[2,1024,128]{2,1,0:T(8,128)(2,1)} %bitcast.7, ...), custom_call_target="tpu_custom_call" | custom-call | tf_op jit(solution)/shard_map/pallas_call | solution.py:175
  38.5 32.7 %shard_map.74 = bf16[2,2048,128]{2,1,0:T(8,128)(2,1)} custom-call(s32[2]{0:T(128)} %len_ref.1, bf16[2,2048,128]{2,1,0:T(8,128)(2,1)} %bitcast.6, bf16[2,1024,128]{2,1,0:T(8,128)(2,1)} %get-tuple-element.9.skb, bf16[2,1024,128]{2,1,0:T(8,128)(2,1)} %get-tuple-element.10.svb, bf16[2,1024,128]{2,1,0:T(8,128)(2,1)} %get-tuple-element.11.kcb, ...), custom_call_target="tpu_custom_call" | custom-call | tf_op jit(solution)/shard_map/pallas_call | solution.py:235

commit v2 on v0

v2 whole, which is shorter than its diff:
```python
import functools
import math

import jax
import jax.numpy as jnp
from jax import lax
from jax.experimental import pallas as pl
from jax.experimental.pallas import tpu as pltpu
from jax.sharding import PartitionSpec as P

MESH = pl.DeviceIdType.MESH
HIDDEN = -1e30
F32 = jnp.float32


def scores_of(query, keys):
    return lax.dot_general(query, keys, (((1,), (1,)), ((), ())), preferred_element_type=F32)


def kernel(
    n, slot_ref, len_ref, q_ref, sk_ref, sv_ref, ck_ref, cv_ref, out_ref,
    qv, qx, skb, svb, kcb, vcb, spread_a, spread_b, picked, kx, vx, acc, top, s0, s1, ov,
    local_sem, s_send, s_recv, p1_send, p1_recv, p2_send, p2_recv, x_send, x_recv, y_send, y_recv, out_sem,
):
    me = lax.axis_index("req")
    q = lax.axis_index("qh")
    core = lax.rem(q, 2)
    side = q // 2
    mate = q + 1 - 2 * core
    over = lax.rem(q + 2, 4)
    reqs, rows, dim = q_ref.shape
    per = sk_ref.shape[1]
    span = ck_ref.shape[1]
    half = span // 2
    part = half // 2
    piece = part // n
    depth = n // 2

    def shift(i):
        s = i // 2
        dz = lax.rem(depth // 2 + (s + 1) // 2 * (1 - 2 * lax.rem(s, 2)) + depth, depth)
        return 1 - lax.rem(i, 2), dz

    def target(i):
        dx, dz = shift(i)
        return lax.rem(me // depth + dx, 2) * depth + lax.rem(lax.rem(me, depth) + dz, depth)

    def source(i):
        dx, dz = shift(i)
        return lax.rem(me // depth + dx, 2) * depth + lax.rem(lax.rem(me, depth) + depth - dz, depth)

    def rows_of(h, of_side, index):
        return pl.ds(pl.multiple_of(h * half + of_side * part + index * piece, piece), piece)

    def pair(index):
        return pl.ds(2 * index, 2)

    def each_core(refs, body):
        for c, ref in enumerate(refs):
            @pl.when(core == c)
            def _(ref=ref):
                body(ref)

    def to_req(src, dst, send, recv, index):
        return pltpu.make_async_remote_copy(
            src, dst, send, recv, device_id={"req": index}, device_id_type=MESH
        )

    def to_qh(src, dst, send, recv, index):
        return pltpu.make_async_remote_copy(
            src, dst, send, recv, device_id={"qh": index}, device_id_type=MESH
        )

    spread = (spread_a, spread_b)
    barrier = pltpu.get_barrier_semaphore()

    def greet(i, _):
        pl.semaphore_signal(barrier, inc=1, device_id={"req": target(i)}, device_id_type=MESH)
        return 0

    lax.fori_loop(0, n - 1, greet, 0)
    for peer in (over, mate):
        pl.semaphore_signal(barrier, inc=1, device_id={"qh": peer}, device_id_type=MESH)

    own = pl.ds(pl.multiple_of(q * per, per), per)
    load_q = pltpu.make_async_copy(q_ref, qv, local_sem.at[0])
    own_copies = [
        pltpu.make_async_copy(sk_ref, skb.at[:, own], local_sem.at[1]),
        pltpu.make_async_copy(sv_ref, svb.at[:, own], local_sem.at[2]),
    ]

    pl.semaphore_wait(barrier, n + 1)

    def spread_out(src):
        for h in range(2):
            def send(i, _, h=h):
                to = target(i)
                to_req(
                    src.at[:, rows_of(h, side, to)], spread[h].at[pair(me)], p1_send, p1_recv.at[h], to
                ).start()
                return 0

            lax.fori_loop(0, n - 1, send, 0)
            pltpu.make_async_copy(
                src.at[:, rows_of(h, side, me)], spread[h].at[pair(me)], local_sem.at[3 + h]
            ).start()

    each_core((ck_ref, cv_ref), spread_out)

    def stretch_to(k, peer):
        return [
            to_qh(src, dst.at[:, own], s_send.at[k, i], s_recv.at[k, i], peer)
            for i, (src, dst) in enumerate(((sk_ref, skb), (sv_ref, svb)))
        ]

    to_over = stretch_to(0, over)
    to_mate = stretch_to(1, mate)
    for copy in to_over + to_mate + [load_q] + own_copies:
        copy.start()

    scale = math.log2(math.e) / math.sqrt(dim)
    load_q.wait()
    block = 256

    def widen(i, _):
        at = pl.ds(pl.multiple_of(i * block, block), block)
        for j in range(reqs):
            value = qv[j, at, :].astype(F32) * scale
            high = value.astype(jnp.bfloat16)
            qx[j, at, :dim] = high
            qx[j, at, dim:] = (value - high.astype(F32)).astype(jnp.bfloat16)
        return 0

    lax.fori_loop(0, rows // block, widen, 0)

    most = pl.ds(0, 2 * (n - 1))

    def collect(h):
        pltpu.make_async_copy(spread[h].at[pair(me)], spread[h].at[pair(me)], local_sem.at[3 + h]).wait()
        pltpu.make_async_copy(spread[h].at[most], spread[h].at[most], p1_recv.at[h]).wait()
        for r in range(2 * n):
            picked[h, r] = spread[h][slot_ref[r]]

        def send_all(dst):
            def send(i, _):
                to = target(i)
                to_req(
                    picked.at[h, pair(to)], dst.at[:, rows_of(h, side, me)], p2_send, p2_recv.at[h, i], to
                ).start()
                return 0

            lax.fori_loop(0, n - 1, send, 0)
            pltpu.make_async_copy(
                picked.at[h, pair(me)], dst.at[:, rows_of(h, side, me)], p2_recv.at[h, n - 1]
            ).start()

        each_core((kcb, vcb), send_all)

    def forward(h):
        def send_all(dst):
            def send(k, _):
                i = n - 1 - k
                at = rows_of(h, side, source(i))
                pltpu.make_async_copy(picked.at[h, pair(0)], dst.at[:, at], p2_recv.at[h, i]).wait()
                to_qh(dst.at[:, at], dst.at[:, at], x_send, x_recv.at[h, i], over).start()
                to_qh(dst.at[:, at], dst.at[:, at], y_send, y_recv.at[h], mate).start()
                return 0

            lax.fori_loop(0, n, send, 0)

        each_core((kcb, vcb), send_all)

    def onward(h):
        def send_all(dst):
            def send(k, _):
                i = n - 1 - k
                at = rows_of(h, 1 - side, source(i))
                pltpu.make_async_copy(picked.at[h, pair(0)], dst.at[:, at], x_recv.at[h, i]).wait()
                to_qh(dst.at[:, at], dst.at[:, at], y_send, y_recv.at[h], mate).start()
                return 0

            lax.fori_loop(0, n, send, 0)

        each_core((kcb, vcb), send_all)

    tile = 512
    tokens = tile // 2

    def stretch_attention(j):
        for i in range(rows // tile):
            at = pl.ds(i * tile, tile)
            seen = (i + 1) * tokens
            keys = skb[j, :seen, :]
            scores = scores_of(qx[j, at, :], jnp.concatenate([keys, keys], axis=1))
            row = lax.broadcasted_iota(jnp.int32, (tile, tokens), 0) // 2
            col = lax.broadcasted_iota(jnp.int32, (tile, tokens), 1)
            last = jnp.where(col <= row, scores[:, seen - tokens:], HIDDEN)
            scores = jnp.concatenate([scores[:, : seen - tokens], last], axis=1) if i else last
            most = jnp.max(scores, axis=1, keepdims=True)
            weights = jnp.exp2(scores - most).astype(jnp.bfloat16)
            values = svb[j, :seen, :]
            wide = jnp.concatenate([values, jnp.ones_like(values)], axis=1)
            acc[j, at, :] = jnp.dot(weights, wide, preferred_element_type=F32)
            top[j, at, :] = jnp.broadcast_to(most, (tile, dim))

    def prepare(h):
        for j in range(reqs):
            at = pl.ds(h * half, half)
            place = h * half + lax.broadcasted_iota(jnp.int32, (half, dim), 0)
            visible = place < len_ref[j]
            first = kcb[j, 0:1, :].astype(F32)
            keys = jnp.where(visible, kcb[j, at, :].astype(F32), first).astype(jnp.bfloat16)
            kx[j, :, :dim] = keys
            kx[j, :, dim:] = keys
            vx[j, :, :dim] = jnp.where(visible, vcb[j, at, :].astype(F32), 0.0).astype(jnp.bfloat16)
            vx[j, :, dim:] = jnp.where(visible, 1.0, 0.0).astype(jnp.bfloat16)

    big = 1024
    tiles = rows // big

    def place_of(t):
        return t // tiles, pl.ds(pl.multiple_of(lax.rem(t, tiles) * big, big), big)

    def cached_scores(t, dst):
        j, at = place_of(t)
        dst[...] = scores_of(qx[j, at, :], kx[j])

    def finish(t, src, last):
        j, at = place_of(t)
        scores = src[...]
        before = top[j, at, :]
        now = jnp.maximum(before, jnp.max(scores, axis=1, keepdims=True))
        weights = jnp.exp2(scores - now[:, :1]).astype(jnp.bfloat16)
        fade = jnp.exp2(before - now)
        mixed = jnp.dot(weights, vx[j], preferred_element_type=F32)
        number = acc[j, at, :dim] * fade + mixed[:, :dim]
        total = acc[j, at, dim:] * fade + mixed[:, dim:]
        if last:
            ov[j, at, :] = (number / total).astype(ov.dtype)
        else:
            acc[j, at, :dim] = number
            acc[j, at, dim:] = total
            top[j, at, :] = now

    def cached_attention(h, between=None):
        count = reqs * tiles
        bufs = (s0, s1)
        cached_scores(0, s0)
        for t in range(count):
            if t + 1 < count:
                cached_scores(t + 1, bufs[(t + 1) % 2])
            finish(t, bufs[t % 2], h == 1)
            if between is not None and t == count // 2 - 1:
                between()
            if h == 1:
                j, at = t // tiles, pl.ds(t % tiles * big, big)
                pltpu.make_async_copy(ov.at[j, at], out_ref.at[j, at], out_sem).start()

    collect(0)
    for copy in to_over:
        copy.wait_recv()
    theirs = pl.ds(pl.multiple_of(over * per, per), per)
    passed = [
        to_qh(dst.at[:, theirs], dst.at[:, theirs], s_send.at[2, i], s_recv.at[2, i], mate)
        for i, dst in enumerate((skb, svb))
    ]
    for copy in passed:
        copy.start()
    collect(1)
    for copy in own_copies:
        copy.wait()
    for copy in to_mate + passed:
        copy.wait_recv()
    stretch_attention(0)
    forward(0)
    stretch_attention(1)
    onward(0)
    forward(1)
    firsts = pl.ds(0, half)
    pltpu.make_async_copy(kcb.at[:, firsts], vcb.at[:, firsts], y_recv.at[0]).wait()
    prepare(0)
    cached_attention(0, lambda: onward(1))
    pltpu.make_async_copy(kcb.at[:, firsts], vcb.at[:, firsts], y_recv.at[1]).wait()
    prepare(1)
    cached_attention(1)

    for copy in to_over + to_mate + passed:
        copy.wait_send()
    for sem in (p1_send, p2_send):
        pltpu.make_async_copy(picked.at[:, most], picked.at[:, most], sem).wait()
    pltpu.make_async_copy(picked, picked, x_send).wait()
    pltpu.make_async_copy(kcb, kcb, y_send).wait()
    pltpu.make_async_copy(ov, out_ref, out_sem).wait()


def attend(slot_of_req, cache_len, queries, stretch_keys, stretch_values, cache_keys, cache_values, n):
    reqs, rows, dim = queries.shape
    span = cache_keys.shape[1]
    half = span // 2
    piece = half // 2 // n
    kind = queries.dtype
    any_spec = pl.BlockSpec(memory_space=pl.ANY)
    smem = pl.BlockSpec(memory_space=pltpu.SMEM)
    dma = pltpu.SemaphoreType.DMA
    vmem = pltpu.VMEM
    return pl.pallas_call(
        functools.partial(kernel, n),
        out_shape=jax.ShapeDtypeStruct(queries.shape, kind),
        in_specs=[smem] * 2 + [any_spec] * 5,
        out_specs=any_spec,
        scratch_shapes=[
            vmem((reqs, rows, dim), kind),
            vmem((reqs, rows, 2 * dim), kind),
            vmem((reqs, span, dim), kind), vmem((reqs, span, dim), kind),
            vmem((reqs, span, dim), kind), vmem((reqs, span, dim), kind),
            vmem((2 * n, piece, dim), kind), vmem((2 * n, piece, dim), kind), vmem((2, 2 * n, piece, dim), kind),
            vmem((reqs, half, 2 * dim), kind), vmem((reqs, half, 2 * dim), kind),
            vmem((reqs, rows, 2 * dim), F32), vmem((reqs, rows, dim), F32),
            vmem((1024, half), F32), vmem((1024, half), F32),
            vmem((reqs, rows, dim), kind),
            dma((5,)), dma((3, 2)), dma((3, 2)), dma, dma((2,)), dma, dma((2, n)),
            dma, dma((2, n)), dma, dma((2,)), dma,
        ],
        compiler_params=pltpu.CompilerParams(collective_id=0, has_side_effects=True),
    )(slot_of_req, cache_len, queries, stretch_keys, stretch_values, cache_keys, cache_values)


def on_device(queries, stretch_keys, stretch_values, cache_keys, cache_values, slot_of_req, cache_len):
    reqs, stretch, heads, dim = queries.shape
    flat = [a.reshape(a.shape[0], a.shape[1], dim) for a in (stretch_keys, stretch_values, cache_keys, cache_values)]
    rows = queries.reshape(reqs, stretch * heads, dim)
    out = attend(slot_of_req, cache_len, rows, *flat, lax.axis_size("req"))
    return out.reshape(queries.shape)


def solution(mesh):
    return jax.shard_map(
        on_device,
        mesh=mesh,
        in_specs=(
            P("req", None, ("kvh", "qh"), None),
            P("req", "qh", "kvh", None),
            P("req", "qh", "kvh", None),
            P("req", None, "kvh", None),
            P("req", None, "kvh", None),
            P(),
            P("req"),
        ),
        out_specs=P("req", None, ("kvh", "qh"), None),
        check_vma=False,
    )
```

time: 174 us -> 49.6 us (0.29)
  Pallas kernels: 0 us -> 46.5 us
  blocking collectives: 40.7 us -> 0 us
  waiting for transfers between devices: 25.1 us -> 0 us
  starting transfers between devices: 24.3 us -> 0 us
  matrix products: 23.7 us -> 0 us
  loops' own time: 21.7 us -> 0 us
  local copies, waits for them, and re-layouts: 22 us -> 2.91 us
  other arithmetic: 15.1 us -> 0 us
    pallas_call x0 -> x1, Pallas kernels: none -> 46.5 us  [attend(): pl.pallas_call(functools.partial(kernel, n), out_shape=jax.ShapeDtypeStru...]
    all_to_all x3 -> x0, waiting for transfers between devices: 25.1 us -> none  [the longest x1 12.9 us: relocate(): lax.all_to_all(split_keys, 'req', split_axis=1, concat_axis=0, tiled=True)]
    all_to_all x3 -> x0, starting transfers between devices: 24.3 us -> none  [the longest x1 11.9 us: relocate(): lax.all_to_all(split_keys, 'req', split_axis=1, concat_axis=0, tiled=True)]
    dot_general x32 -> x0, matrix products: 23.7 us -> none  [the longest x8 10.5 us: one_block(): jnp.dot(weight_n.astype(jnp.bfloat16), value_n, preferred_element_type=jn...]
    all_gather x2 -> x0, blocking collectives: 21.9 us -> none  [the longest x1 12.7 us: on_device(): lax.all_gather(stretch_keys, 'qh', axis=1, tiled=True)]
    another operation x1 -> x0, loops' own time: 21.7 us -> none  [on_device(): results = lax.map(one_block, jnp.arange(count, dtype=jnp.int32))]
    all_to_all x1 -> x0, blocking collectives: 18.8 us -> none  [relocate(): lax.all_to_all(picked_keys, 'req', split_axis=0, concat_axis=1, tiled=True)]
    dynamic_slice x16 -> x0, local copies, waits for them, and re-layouts: 9.37 us -> none  [the longest x8 4.71 us: one_block(): length = lax.dynamic_index_in_dim(cache_len, request, 0, keepdims=False)]
  transfers between devices with their start and end apart: 3 -> 0, of which waited for: 2 -> 0; matrix products, arithmetic and copies ran while one was open for 2% -> 0% of each run, Pallas kernels for 0% -> 0%
where the time goes in v2:
time: 49.6 us; the launch traced here: 49.4 us
  Pallas kernels  46.5 us (94%)
  local copies, waits for them, and re-layouts  2.91 us (6%)
    pallas_call x1, Pallas kernels, attend(): pl.pallas_call(functools.partial(kernel, n), out_shape=jax.ShapeDtypeStru...  46.5 us
    unnamed x1, local copies, waits for them, and re-layouts  2.91 us

profile of v2, /device:TPU:1, one launch (start us, length us, event | category | flops | bytes accessed | tf_op | source)
XLA Modules:
  0.0 49.4 jit_solution(15406499262016932780)
XLA Ops:
  0.0 46.5 %shard_map.73 = bf16[2,2048,128]{2,1,0:T(8,128)(2,1)} custom-call(s32[32]{0:T(128)} %slot_ref.1, s32[2]{0:T(128)} %len_ref.1, bf16[2,2048,128]{2,1,0:T(8,128)(2,1)} %bitcast.7, bf16[2,256,128]{2,1,0:T(8,128)(2,1)} %bitcast.10, bf16[2,256,128]{2,1,0:T(8,128)(2,1)} %bitcast.11, bf16[2,1024,128]{2,1,0:T(8,128)(2,1)} %bitcast.8, bf16[2,1024,128]{2,1,0:T(8,128)(2,1)} %bitcast.9), custom_call_target="tpu_custom_call" | custom-call | tf_op jit(solution)/shard_map/pallas_call | solution.py:306
  46.5 2.9 %copy.9 = bf16[2,1024,2,128]{3,2,1,0:T(2,128)(2,1)} copy(bf16[2,1024,2,128]{3,2,1,0:T(2,128)(2,1)} %bitcast.6) | data formatting | bytes 2097152

commit v3 on v2

v3 whole, which is shorter than its diff:
```python
import functools
import math

import jax
import jax.numpy as jnp
from jax import lax
from jax.experimental import pallas as pl
from jax.experimental.pallas import tpu as pltpu
from jax.sharding import PartitionSpec as P

MESH = pl.DeviceIdType.MESH
HIDDEN = -1e30
F32 = jnp.float32


def scores_of(query, keys):
    return lax.dot_general(query, keys, (((1,), (1,)), ((), ())), preferred_element_type=F32)


def prepare(h, j, len_ref, kvb, kx, vx):
    half, dim = kx.shape[1], kx.shape[2] // 2
    at = pl.ds(h * half, half)
    place = h * half + lax.broadcasted_iota(jnp.int32, (half, dim), 0)
    visible = place < len_ref[j]
    first = kvb[0, j, 0:1, :].astype(F32)
    keys = jnp.where(visible, kvb[0, j, at, :].astype(F32), first).astype(jnp.bfloat16)
    kx[j, :, :dim] = keys
    kx[j, :, dim:] = keys
    vx[j, :, :dim] = jnp.where(visible, kvb[1, j, at, :].astype(F32), 0.0).astype(jnp.bfloat16)
    vx[j, :, dim:] = jnp.where(visible, 1.0, 0.0).astype(jnp.bfloat16)


def join(scores, before, values):
    now = jnp.maximum(before, jnp.max(scores, axis=1, keepdims=True))
    weights = jnp.exp2(scores - now[:, :1]).astype(jnp.bfloat16)
    return now, jnp.exp2(before - now), jnp.dot(weights, values, preferred_element_type=F32)


def kernel(
    n, slot_ref, len_ref, q_ref, sk_ref, sv_ref, ck_ref, cv_ref, qx, acc, top, kvb,
    qv, skb, svb, spread_a, spread_b, picked, kx, vx, s0, s1,
    local_sem, s_send, s_recv, p1_send, p1_recv, p2_send, p2_recv, x_send, x_recv, y_send, y_recv,
):
    me = lax.axis_index("req")
    q = lax.axis_index("qh")
    core = lax.rem(q, 2)
    side = q // 2
    mate = q + 1 - 2 * core
    over = lax.rem(q + 2, 4)
    reqs, rows, dim = q_ref.shape
    per = sk_ref.shape[1]
    span = ck_ref.shape[1]
    half = span // 2
    part = half // 2
    piece = part // n
    depth = n // 2

    far = sorted(range(depth), key=lambda dz: -min(dz, depth - dz))
    offsets = [(dx, dz) for dz in far for dx in (1, 0) if dx or dz]
    all_offsets = offsets + [(0, 0)]
    here = side * 2 + me // depth
    up = here + 1 - 2 * lax.rem(here, 2)
    down = lax.rem(here + 3 + 2 * lax.rem(here, 2), 4)
    columns = [(x // 2, lax.rem(x, 2) * depth) for x in (here, up, down)]
    heights = [lax.rem(lax.rem(me, depth) + dz, depth) for dz in range(depth)]

    def partner(offset, sign):
        dx, dz = offset
        of_side, base = columns[dx * (1 + dz % 2)]
        return of_side, base + heights[sign * dz % depth]

    def rows_of(h, of_side, index):
        return pl.ds(pl.multiple_of(h * half + of_side * part + index * piece, piece), piece)

    def pair(index):
        return pl.ds(2 * index, 2)

    def to_req(src, dst, send, recv, of_side, index):
        return pltpu.make_async_remote_copy(
            src, dst, send, recv, device_id={"qh": of_side * 2 + core, "req": index}, device_id_type=MESH
        )

    def to_qh(src, dst, send, recv, index):
        return pltpu.make_async_remote_copy(
            src, dst, send, recv, device_id={"qh": index}, device_id_type=MESH
        )

    spread = (spread_a, spread_b)
    barrier = pltpu.get_barrier_semaphore()
    for offset in offsets:
        of_side, index = partner(offset, 1)
        pl.semaphore_signal(
            barrier, inc=1, device_id={"qh": of_side * 2 + core, "req": index}, device_id_type=MESH
        )
    for peer in (over, mate):
        pl.semaphore_signal(barrier, inc=1, device_id={"qh": peer}, device_id_type=MESH)

    own = pl.ds(pl.multiple_of(q * per, per), per)
    load_q = pltpu.make_async_copy(q_ref, qv, local_sem.at[0])
    own_copies = [
        pltpu.make_async_copy(sk_ref, skb.at[:, own], local_sem.at[1]),
        pltpu.make_async_copy(sv_ref, svb.at[:, own], local_sem.at[2]),
    ]

    pl.semaphore_wait(barrier, n + 1)

    for c, src in enumerate((ck_ref, cv_ref)):
        @pl.when(core == c)
        def _(src=src):
            for h in range(2):
                for offset in offsets:
                    of_side, to = partner(offset, 1)
                    to_req(
                        src.at[:, rows_of(h, of_side, to)], spread[h].at[pair(me)], p1_send, p1_recv.at[h],
                        of_side, to,
                    ).start()
                pltpu.make_async_copy(
                    src.at[:, rows_of(h, side, me)], spread[h].at[pair(me)], local_sem.at[3 + h]
                ).start()

    def stretch_to(k, peer):
        return [
            to_qh(src, dst.at[:, own], s_send.at[k, i], s_recv.at[k, i], peer)
            for i, (src, dst) in enumerate(((sk_ref, skb), (sv_ref, svb)))
        ]

    to_over = stretch_to(0, over)
    to_mate = stretch_to(1, mate)
    for copy in to_over + to_mate + [load_q] + own_copies:
        copy.start()

    scale = math.log2(math.e) / math.sqrt(dim)
    load_q.wait()
    block = 256

    def widen(i, _):
        at = pl.ds(pl.multiple_of(i * block, block), block)
        for j in range(reqs):
            value = qv[j, at, :].astype(F32) * scale
            high = value.astype(jnp.bfloat16)
            qx[j, at, :dim] = high
            qx[j, at, dim:] = (value - high.astype(F32)).astype(jnp.bfloat16)
        return 0

    lax.fori_loop(0, rows // block, widen, 0)

    most = pl.ds(0, 2 * (n - 1))

    def collect(h):
        pltpu.make_async_copy(spread[h].at[pair(me)], spread[h].at[pair(me)], local_sem.at[3 + h]).wait()
        pltpu.make_async_copy(spread[h].at[most], spread[h].at[most], p1_recv.at[h]).wait()
        for r in range(2 * n):
            picked[h, r] = spread[h][slot_ref[r]]
        dst = kvb.at[core, :, rows_of(h, side, me)]
        for i, offset in enumerate(offsets):
            of_side, to = partner(offset, 1)
            to_req(picked.at[h, pair(to)], dst, p2_send, p2_recv.at[h, i], of_side, to).start()
        pltpu.make_async_copy(picked.at[h, pair(me)], dst, p2_recv.at[h, n - 1]).start()

    def forward(h):
        for i in reversed(range(n)):
            of_side, index = partner(all_offsets[i], -1)
            at = kvb.at[core, :, rows_of(h, of_side, index)]
            pltpu.make_async_copy(picked.at[h, pair(0)], at, p2_recv.at[h, i]).wait()
            to_qh(at, at, x_send, x_recv.at[h, i], over).start()
            to_qh(at, at, y_send, y_recv.at[h], mate).start()

    def onward(h):
        for i in reversed(range(n)):
            of_side, index = partner(all_offsets[i], -1)
            at = kvb.at[core, :, rows_of(h, 1 - of_side, index)]
            pltpu.make_async_copy(picked.at[h, pair(0)], at, x_recv.at[h, i]).wait()
            to_qh(at, at, y_send, y_recv.at[h], mate).start()

    tile = 512
    tokens = tile // 2

    def stretch_attention(j):
        for i in range(rows // tile):
            at = pl.ds(i * tile, tile)
            seen = (i + 1) * tokens
            keys = skb[j, :seen, :]
            scores = scores_of(qx[j, at, :], jnp.concatenate([keys, keys], axis=1))
            row = lax.broadcasted_iota(jnp.int32, (tile, tokens), 0) // 2
            col = lax.broadcasted_iota(jnp.int32, (tile, tokens), 1)
            last = jnp.where(col <= row, scores[:, seen - tokens:], HIDDEN)
            scores = jnp.concatenate([scores[:, : seen - tokens], last], axis=1) if i else last
            highest = jnp.max(scores, axis=1, keepdims=True)
            weights = jnp.exp2(scores - highest).astype(jnp.bfloat16)
            values = svb[j, :seen, :]
            wide = jnp.concatenate([values, jnp.ones_like(values)], axis=1)
            acc[j, at, :] = jnp.dot(weights, wide, preferred_element_type=F32)
            top[j, at, :] = jnp.broadcast_to(highest, (tile, dim))

    big = 1024
    count = reqs * rows // big

    def place_of(t):
        return t // (rows // big), pl.ds(t % (rows // big) * big, big)

    def cached_scores(t):
        j, at = place_of(t)
        (s0, s1)[t % 2][...] = scores_of(qx[j, at, :], kx[j])

    def cached_attention(first, stop):
        for t in range(first, stop):
            if t + 1 < count:
                cached_scores(t + 1)
            j, at = place_of(t)
            now, fade, mixed = join((s0, s1)[t % 2][...], top[j, at, :], vx[j])
            acc[j, at, :dim] = acc[j, at, :dim] * fade + mixed[:, :dim]
            acc[j, at, dim:] = acc[j, at, dim:] * fade + mixed[:, dim:]
            top[j, at, :] = now

    collect(0)
    for copy in to_over:
        copy.wait_recv()
    theirs = pl.ds(pl.multiple_of(over * per, per), per)
    passed = [
        to_qh(dst.at[:, theirs], dst.at[:, theirs], s_send.at[2, i], s_recv.at[2, i], mate)
        for i, dst in enumerate((skb, svb))
    ]
    for copy in passed:
        copy.start()
    collect(1)
    for copy in own_copies:
        copy.wait()
    for copy in to_mate + passed:
        copy.wait_recv()
    stretch_attention(0)
    forward(0)
    stretch_attention(1)
    forward(1)
    onward(0)
    firsts = pl.ds(0, half)
    pltpu.make_async_copy(kvb.at[0, :, firsts], kvb.at[0, :, firsts], y_recv.at[0]).wait()
    for j in range(reqs):
        prepare(0, j, len_ref, kvb, kx, vx)
    cached_scores(0)
    cached_attention(0, count // 2)
    onward(1)
    cached_attention(count // 2, count)
    pltpu.make_async_copy(kvb.at[0, :, firsts], kvb.at[0, :, firsts], y_recv.at[1]).wait()

    for copy in to_over + to_mate + passed:
        copy.wait_send()
    for sem in (p1_send, p2_send):
        pltpu.make_async_copy(picked.at[:, most], picked.at[:, most], sem).wait()
    pltpu.make_async_copy(picked, picked, x_send).wait()
    pltpu.make_async_copy(kvb.at[0], kvb.at[0], y_send).wait()


def finish_kernel(len_ref, qx, acc, top, kvb, out_ref, kx, vx, s0, s1, ov, sem):
    reqs, rows, dim = ov.shape
    half = kx.shape[1]
    tile = 512
    bufs = (s0, s1)
    for j in range(reqs):
        def scores(t, j=j):
            bufs[t % 2][...] = scores_of(qx[j, pl.ds(t * tile, tile), :], kx[j])

        def put(at, number, total, j=j):
            ov[j, at, :] = (number / total).astype(ov.dtype)
            pltpu.make_async_copy(ov.at[j, at], out_ref.at[j, at], sem).start()

        @pl.when(len_ref[j] > half)
        def _(j=j, scores=scores, put=put):
            prepare(1, j, len_ref, kvb, kx, vx)
            scores(0)
            for t in range(rows // tile):
                if t + 1 < rows // tile:
                    scores(t + 1)
                at = pl.ds(t * tile, tile)
                _, fade, mixed = join(bufs[t % 2][...], top[j, at, :], vx[j])
                put(at, acc[j, at, :dim] * fade + mixed[:, :dim], acc[j, at, dim:] * fade + mixed[:, dim:])

        @pl.when(len_ref[j] <= half)
        def _(j=j, put=put):
            for t in range(rows // tile):
                at = pl.ds(t * tile, tile)
                put(at, acc[j, at, :dim], acc[j, at, dim:])

    pltpu.make_async_copy(ov, out_ref, sem).wait()


def attend(slot_of_req, cache_len, queries, stretch_keys, stretch_values, cache_keys, cache_values, n):
    reqs, rows, dim = queries.shape
    span = cache_keys.shape[1]
    half = span // 2
    piece = half // 2 // n
    kind = queries.dtype
    any_spec = pl.BlockSpec(memory_space=pltpu.HBM)
    smem = pl.BlockSpec(memory_space=pltpu.SMEM)
    dma = pltpu.SemaphoreType.DMA
    vmem = pltpu.VMEM
    held = pl.BlockSpec(memory_space=vmem)
    state = (
        vmem((reqs, rows, 2 * dim), kind),
        vmem((reqs, rows, 2 * dim), F32), vmem((reqs, rows, dim), F32),
        vmem((2, reqs, span, dim), kind),
    )
    limit = 57_600_000
    state = pl.pallas_call(
        functools.partial(kernel, n),
        out_shape=state,
        in_specs=[smem] * 2 + [any_spec] * 5,
        out_specs=(held,) * len(state),
        scratch_shapes=[
            vmem((reqs, rows, dim), kind),
            vmem((reqs, span, dim), kind), vmem((reqs, span, dim), kind),
            vmem((2 * n, piece, dim), kind), vmem((2 * n, piece, dim), kind), vmem((2, 2 * n, piece, dim), kind),
            vmem((reqs, half, 2 * dim), kind), vmem((reqs, half, 2 * dim), kind),
            vmem((1024, half), F32), vmem((1024, half), F32),
            dma((5,)), dma((3, 2)), dma((3, 2)), dma, dma((2,)), dma, dma((2, n)),
            dma, dma((2, n)), dma, dma((2,)),
        ],
        compiler_params=pltpu.CompilerParams(collective_id=0, has_side_effects=True, vmem_limit_bytes=limit),
    )(slot_of_req, cache_len, queries, stretch_keys, stretch_values, cache_keys, cache_values)
    state = [pltpu.with_memory_space_constraint(a, vmem) for a in state]
    return pl.pallas_call(
        finish_kernel,
        out_shape=jax.ShapeDtypeStruct(queries.shape, kind),
        in_specs=[smem] + [held] * len(state),
        out_specs=any_spec,
        scratch_shapes=[
            vmem((reqs, half, 2 * dim), kind), vmem((reqs, half, 2 * dim), kind),
            vmem((512, half), F32), vmem((512, half), F32),
            vmem((reqs, rows, dim), kind), dma,
        ],
        compiler_params=pltpu.CompilerParams(vmem_limit_bytes=limit),
    )(cache_len, *state)


def on_device(queries, stretch_keys, stretch_values, cache_keys, cache_values, slot_of_req, cache_len):
    reqs, stretch, heads, dim = queries.shape
    flat = [a.reshape(a.shape[0], a.shape[1], dim) for a in (stretch_keys, stretch_values, cache_keys, cache_values)]
    rows = queries.reshape(reqs, stretch * heads, dim)
    out = attend(slot_of_req, cache_len, rows, *flat, lax.axis_size("req"))
    return out.reshape(queries.shape)


def solution(mesh):
    return jax.shard_map(
        on_device,
        mesh=mesh,
        in_specs=(
            P("req", None, ("kvh", "qh"), None),
            P("req", "qh", "kvh", None),
            P("req", "qh", "kvh", None),
            P("req", None, "kvh", None),
            P("req", None, "kvh", None),
            P(),
            P("req"),
        ),
        out_specs=P("req", None, ("kvh", "qh"), None),
        check_vma=False,
    )
```

time: 49.6 us -> 43.7 us (0.88); the launches traced: 49.4 us -> 43 us
  Pallas kernels: 46.5 us -> 42.8 us
  local copies, waits for them, and re-layouts: 2.91 us -> 0 us
    pallas_call x1 -> x2, Pallas kernels: 46.5 us -> 42.8 us  [the longest x1 39 us: attend(): pl.pallas_call(functools.partial(kernel, n), out_shape=state, in_specs=[s...]
    unnamed x1 -> x0, local copies, waits for them, and re-layouts: 2.91 us -> none
where the time goes in v3:
time: 43.7 us; the launch traced here: 43 us
  Pallas kernels  42.8 us (98%)
    pallas_call x1, Pallas kernels, attend(): pl.pallas_call(functools.partial(kernel, n), out_shape=state, in_specs=[s...  39 us
    pallas_call x1, Pallas kernels, attend(): pl.pallas_call(finish_kernel, out_shape=jax.ShapeDtypeStruct(queries.shap...  3.81 us

profile of v3, /device:TPU:1, one launch (start us, length us, event | category | flops | bytes accessed | tf_op | source)
XLA Modules:
  0.0 43.0 jit_solution(11426909778224724077)
XLA Ops:
  0.0 39.0 %shard_map.73 = (bf16[2,2048,256]{2,1,0:T(8,128)(2,1)S(1)}, f32[2,2048,256]{2,1,0:T(8,128)S(1)}, f32[2,2048,128]{2,1,0:T(8,128)S(1)}, bf16[2,2,1024,128]{3,2,1,0:T(8,128)(2,1)S(1)}) custom-call(s32[32]{0:T(128)} %slot_ref.1, s32[2]{0:T(128)} %len_ref.3, bf16[2,2048,128]{2,1,0:T(8,128)(2,1)} %bitcast.6, bf16[2,256,128]{2,1,0:T(8,128)(2,1)} %bitcast.9, ...), custom_call_target="tpu_custom_call" | custom-call | tf_op jit(solution)/shard_map/pallas_call | solution.py:303
  39.0 3.8 %shard_map.74 = bf16[2,2048,128]{2,1,0:T(8,128)(2,1)} custom-call(s32[2]{0:T(128)} %len_ref.3, bf16[2,2048,256]{2,1,0:T(8,128)(2,1)S(1)} %get-tuple-element.9.qx, f32[2,2048,256]{2,1,0:T(8,128)S(1)} %get-tuple-element.10.acc, f32[2,2048,128]{2,1,0:T(8,128)S(1)} %get-tuple-element.11.top, bf16[2,2,1024,128]{3,2,1,0:T(8,128)(2,1)S(1)} %get-tuple-element.12.kvb), custom_call_target="tpu_custom_call" | custom-call | tf_op jit(solution)/shard_map/pallas_call | solution.py:320

commit v4 on v3

--- a/solution.py
+++ b/solution.py
@@ -13,33 +13,40 @@
 F32 = jnp.float32
 
 
+CHUNKS = (4, 2, 2)
+
+
 def scores_of(query, keys):
     return lax.dot_general(query, keys, (((1,), (1,)), ((), ())), preferred_element_type=F32)
 
 
-def prepare(h, j, len_ref, kvb, kx, vx):
-    half, dim = kx.shape[1], kx.shape[2] // 2
-    at = pl.ds(h * half, half)
-    place = h * half + lax.broadcasted_iota(jnp.int32, (half, dim), 0)
-    visible = place < len_ref[j]
-    first = kvb[0, j, 0:1, :].astype(F32)
-    keys = jnp.where(visible, kvb[0, j, at, :].astype(F32), first).astype(jnp.bfloat16)
+def mark(start, j, len_ref, vx):
+    size, dim = vx.shape[1], vx.shape[2] // 2
+    place = start + lax.broadcasted_iota(jnp.int32, (size, dim), 0)
+    vx[j, :, dim:] = jnp.where(place < len_ref[j], 1.0, 0.0).astype(jnp.bfloat16)
+
+
+def prepare(start, j, kvb, kx, vx):
+    size, dim = kx.shape[1], kx.shape[2] // 2
+    at = pl.ds(start, size)
+    visible = vx[j, :, dim:]
+    keys = kvb[0, j, at, :] * visible + kvb[0, j, 0:1, :] * (1 - visible)
     kx[j, :, :dim] = keys
     kx[j, :, dim:] = keys
-    vx[j, :, :dim] = jnp.where(visible, kvb[1, j, at, :].astype(F32), 0.0).astype(jnp.bfloat16)
-    vx[j, :, dim:] = jnp.where(visible, 1.0, 0.0).astype(jnp.bfloat16)
+    vx[j, :, :dim] = kvb[1, j, at, :] * visible
 
 
 def join(scores, before, values):
     now = jnp.maximum(before, jnp.max(scores, axis=1, keepdims=True))
-    weights = jnp.exp2(scores - now[:, :1]).astype(jnp.bfloat16)
+    wide = jnp.concatenate([now] * (scores.shape[1] // now.shape[1]), axis=1)
+    weights = jnp.exp2(scores - wide).astype(jnp.bfloat16)
     return now, jnp.exp2(before - now), jnp.dot(weights, values, preferred_element_type=F32)
 
 
 def kernel(
     n, slot_ref, len_ref, q_ref, sk_ref, sv_ref, ck_ref, cv_ref, qx, acc, top, kvb,
-    qv, skb, svb, spread_a, spread_b, picked, kx, vx, s0, s1,
-    local_sem, s_send, s_recv, p1_send, p1_recv, p2_send, p2_recv, x_send, x_recv, y_send, y_recv,
+    qv, skb, svb, s0, s1, spread, picked, kx, vx,
+    local_sem, own_sem, s_send, s_recv, p1_send, p1_recv, p2_send, p2_recv, x_send, x_recv, y_send, y_recv,
 ):
     me = lax.axis_index("req")
     q = lax.axis_index("qh")
@@ -50,9 +57,9 @@
     reqs, rows, dim = q_ref.shape
     per = sk_ref.shape[1]
     span = ck_ref.shape[1]
-    half = span // 2
-    part = half // 2
-    piece = part // n
+    sizes = [span // 8 * c for c in CHUNKS]
+    starts = [sum(sizes[:h]) for h in range(len(sizes))]
+    chunks = range(len(sizes))
     depth = n // 2
 
     far = sorted(range(depth), key=lambda dz: -min(dz, depth - dz))
@@ -70,7 +77,8 @@
         return of_side, base + heights[sign * dz % depth]
 
     def rows_of(h, of_side, index):
-        return pl.ds(pl.multiple_of(h * half + of_side * part + index * piece, piece), piece)
+        piece = sizes[h] // 2 // n
+        return pl.ds(pl.multiple_of(starts[h] + (of_side * n + index) * piece, piece), piece)
 
     def pair(index):
         return pl.ds(2 * index, 2)
@@ -85,7 +93,6 @@
             src, dst, send, recv, device_id={"qh": index}, device_id_type=MESH
         )
 
-    spread = (spread_a, spread_b)
     barrier = pltpu.get_barrier_semaphore()
     for offset in offsets:
         of_side, index = partner(offset, 1)
@@ -107,15 +114,15 @@
     for c, src in enumerate((ck_ref, cv_ref)):
         @pl.when(core == c)
         def _(src=src):
-            for h in range(2):
+            for h in chunks:
                 for offset in offsets:
                     of_side, to = partner(offset, 1)
                     to_req(
-                        src.at[:, rows_of(h, of_side, to)], spread[h].at[pair(me)], p1_send, p1_recv.at[h],
+                        src.at[:, rows_of(h, of_side, to)], spread[h].at[pair(me)], p1_send.at[h], p1_recv.at[h],
                         of_side, to,
                     ).start()
                 pltpu.make_async_copy(
-                    src.at[:, rows_of(h, side, me)], spread[h].at[pair(me)], local_sem.at[3 + h]
+                    src.at[:, rows_of(h, side, me)], spread[h].at[pair(me)], own_sem.at[h]
                 ).start()
 
     def stretch_to(k, peer):
@@ -147,29 +154,29 @@
     most = pl.ds(0, 2 * (n - 1))
 
     def collect(h):
-        pltpu.make_async_copy(spread[h].at[pair(me)], spread[h].at[pair(me)], local_sem.at[3 + h]).wait()
+        pltpu.make_async_copy(spread[h].at[pair(me)], spread[h].at[pair(me)], own_sem.at[h]).wait()
         pltpu.make_async_copy(spread[h].at[most], spread[h].at[most], p1_recv.at[h]).wait()
         for r in range(2 * n):
-            picked[h, r] = spread[h][slot_ref[r]]
+            picked[h][r] = spread[h][slot_ref[r]]
         dst = kvb.at[core, :, rows_of(h, side, me)]
         for i, offset in enumerate(offsets):
             of_side, to = partner(offset, 1)
-            to_req(picked.at[h, pair(to)], dst, p2_send, p2_recv.at[h, i], of_side, to).start()
-        pltpu.make_async_copy(picked.at[h, pair(me)], dst, p2_recv.at[h, n - 1]).start()
+            to_req(picked[h].at[pair(to)], dst, p2_send.at[h], p2_recv.at[h, i], of_side, to).start()
+        pltpu.make_async_copy(picked[h].at[pair(me)], dst, p2_recv.at[h, n - 1]).start()
 
     def forward(h):
         for i in reversed(range(n)):
             of_side, index = partner(all_offsets[i], -1)
             at = kvb.at[core, :, rows_of(h, of_side, index)]
-            pltpu.make_async_copy(picked.at[h, pair(0)], at, p2_recv.at[h, i]).wait()
-            to_qh(at, at, x_send, x_recv.at[h, i], over).start()
+            pltpu.make_async_copy(picked[h].at[pair(0)], at, p2_recv.at[h, i]).wait()
+            to_qh(at, at, x_send.at[h], x_recv.at[h, i], over).start()
             to_qh(at, at, y_send, y_recv.at[h], mate).start()
 
     def onward(h):
         for i in reversed(range(n)):
             of_side, index = partner(all_offsets[i], -1)
             at = kvb.at[core, :, rows_of(h, 1 - of_side, index)]
-            pltpu.make_async_copy(picked.at[h, pair(0)], at, x_recv.at[h, i]).wait()
+            pltpu.make_async_copy(picked[h].at[pair(0)], at, x_recv.at[h, i]).wait()
             to_qh(at, at, y_send, y_recv.at[h], mate).start()
 
     tile = 512
@@ -198,20 +205,23 @@
     def place_of(t):
         return t // (rows // big), pl.ds(t % (rows // big) * big, big)
 
-    def cached_scores(t):
+    def cached_scores(h, t):
         j, at = place_of(t)
-        (s0, s1)[t % 2][...] = scores_of(qx[j, at, :], kx[j])
-
-    def cached_attention(first, stop):
+        (s0, s1)[t % 2][:, : sizes[h]] = scores_of(qx[j, at, :], kx[h][j])
+
+    def cached_attention(h, first, stop):
         for t in range(first, stop):
             if t + 1 < count:
-                cached_scores(t + 1)
+                cached_scores(h, t + 1)
             j, at = place_of(t)
-            now, fade, mixed = join((s0, s1)[t % 2][...], top[j, at, :], vx[j])
+            now, fade, mixed = join((s0, s1)[t % 2][:, : sizes[h]], top[j, at, :], vx[h][j])
             acc[j, at, :dim] = acc[j, at, :dim] * fade + mixed[:, :dim]
             acc[j, at, dim:] = acc[j, at, dim:] * fade + mixed[:, dim:]
             top[j, at, :] = now
 
+    for h in chunks[:-1]:
+        for j in range(reqs):
+            mark(starts[h], j, len_ref, vx[h])
     collect(0)
     for copy in to_over:
         copy.wait_recv()
@@ -222,7 +232,8 @@
     ]
     for copy in passed:
         copy.start()
-    collect(1)
+    for h in chunks[1:]:
+        collect(h)
     for copy in own_copies:
         copy.wait()
     for copy in to_mate + passed:
@@ -230,29 +241,34 @@
     stretch_attention(0)
     forward(0)
     stretch_attention(1)
-    forward(1)
+    for h in chunks[1:]:
+        forward(h)
     onward(0)
-    firsts = pl.ds(0, half)
-    pltpu.make_async_copy(kvb.at[0, :, firsts], kvb.at[0, :, firsts], y_recv.at[0]).wait()
-    for j in range(reqs):
-        prepare(0, j, len_ref, kvb, kx, vx)
-    cached_scores(0)
-    cached_attention(0, count // 2)
-    onward(1)
-    cached_attention(count // 2, count)
-    pltpu.make_async_copy(kvb.at[0, :, firsts], kvb.at[0, :, firsts], y_recv.at[1]).wait()
+    for h in chunks:
+        landed = kvb.at[0, :, pl.ds(starts[h], sizes[h])]
+        pltpu.make_async_copy(landed, landed, y_recv.at[h]).wait()
+        if h == chunks[-1]:
+            break
+        for j in range(reqs):
+            prepare(starts[h], j, kvb, kx[h], vx[h])
+        cached_scores(h, 0)
+        cached_attention(h, 0, count // 2)
+        onward(h + 1)
+        cached_attention(h, count // 2, count)
 
     for copy in to_over + to_mate + passed:
         copy.wait_send()
     for sem in (p1_send, p2_send):
-        pltpu.make_async_copy(picked.at[:, most], picked.at[:, most], sem).wait()
-    pltpu.make_async_copy(picked, picked, x_send).wait()
+        for h in chunks:
+            pltpu.make_async_copy(picked[h].at[most], picked[h].at[most], sem.at[h]).wait()
+    for h in chunks:
+        pltpu.make_async_copy(picked[h], picked[h], x_send.at[h]).wait()
     pltpu.make_async_copy(kvb.at[0], kvb.at[0], y_send).wait()
 
 
 def finish_kernel(len_ref, qx, acc, top, kvb, out_ref, kx, vx, s0, s1, ov, sem):
     reqs, rows, dim = ov.shape
-    half = kx.shape[1]
+    start = kvb.shape[2] - kx.shape[1]
     tile = 512
     bufs = (s0, s1)
     for j in range(reqs):
@@ -263,9 +279,10 @@
             ov[j, at, :] = (number / total).astype(ov.dtype)
             pltpu.make_async_copy(ov.at[j, at], out_ref.at[j, at], sem).start()
 
-        @pl.when(len_ref[j] > half)
+        @pl.when(len_ref[j] > start)
         def _(j=j, scores=scores, put=put):
-            prepare(1, j, len_ref, kvb, kx, vx)
+            mark(start, j, len_ref, vx)
+            prepare(start, j, kvb, kx, vx)
             scores(0)
             for t in range(rows // tile):
                 if t + 1 < rows // tile:
@@ -274,7 +291,7 @@
                 _, fade, mixed = join(bufs[t % 2][...], top[j, at, :], vx[j])
                 put(at, acc[j, at, :dim] * fade + mixed[:, :dim], acc[j, at, dim:] * fade + mixed[:, dim:])
 
-        @pl.when(len_ref[j] <= half)
+        @pl.when(len_ref[j] <= start)
         def _(j=j, put=put):
             for t in range(rows // tile):
                 at = pl.ds(t * tile, tile)
@@ -284,15 +301,17 @@
 
 
 def attend(slot_of_req, cache_len, queries, stretch_keys, stretch_values, cache_keys, cache_values, n):
+    vmem = pltpu.VMEM
     reqs, rows, dim = queries.shape
     span = cache_keys.shape[1]
-    half = span // 2
-    piece = half // 2 // n
+    sizes = [span // 8 * c for c in CHUNKS]
+    pieces = [vmem((2 * n, size // 2 // n, dim), queries.dtype) for size in sizes]
+    wide = [vmem((reqs, size, 2 * dim), queries.dtype) for size in sizes]
+    k = len(sizes)
     kind = queries.dtype
     any_spec = pl.BlockSpec(memory_space=pltpu.HBM)
     smem = pl.BlockSpec(memory_space=pltpu.SMEM)
     dma = pltpu.SemaphoreType.DMA
-    vmem = pltpu.VMEM
     held = pl.BlockSpec(memory_space=vmem)
     state = (
         vmem((reqs, rows, 2 * dim), kind),
@@ -308,11 +327,10 @@
         scratch_shapes=[
             vmem((reqs, rows, dim), kind),
             vmem((reqs, span, dim), kind), vmem((reqs, span, dim), kind),
-            vmem((2 * n, piece, dim), kind), vmem((2 * n, piece, dim), kind), vmem((2, 2 * n, piece, dim), kind),
-            vmem((reqs, half, 2 * dim), kind), vmem((reqs, half, 2 * dim), kind),
-            vmem((1024, half), F32), vmem((1024, half), F32),
-            dma((5,)), dma((3, 2)), dma((3, 2)), dma, dma((2,)), dma, dma((2, n)),
-            dma, dma((2, n)), dma, dma((2,)),
+            vmem((1024, max(sizes)), F32), vmem((1024, max(sizes)), F32),
+            pieces, pieces, wide[:-1], wide[:-1],
+            dma((3,)), dma((k,)), dma((3, 2)), dma((3, 2)), dma((k,)), dma((k,)), dma((k,)), dma((k, n)),
+            dma((k,)), dma((k, n)), dma, dma((k,)),
         ],
         compiler_params=pltpu.CompilerParams(collective_id=0, has_side_effects=True, vmem_limit_bytes=limit),
     )(slot_of_req, cache_len, queries, stretch_keys, stretch_values, cache_keys, cache_values)
@@ -323,8 +341,8 @@
         in_specs=[smem] + [held] * len(state),
         out_specs=any_spec,
         scratch_shapes=[
-            vmem((reqs, half, 2 * dim), kind), vmem((reqs, half, 2 * dim), kind),
-            vmem((512, half), F32), vmem((512, half), F32),
+            wide[-1], wide[-1],
+            vmem((512, sizes[-1]), F32), vmem((512, sizes[-1]), F32),
             vmem((reqs, rows, dim), kind), dma,
         ],
         compiler_params=pltpu.CompilerParams(vmem_limit_bytes=limit),

time: 43.7 us -> 43.9 us (level); the launches traced: 43 us -> 43.7 us
  Pallas kernels: 42.8 us -> 43.7 us
    pallas_call x1, Pallas kernels: 39 us -> 41 us  [attend(): pl.pallas_call(functools.partial(kernel, n), out_shape=state, in_specs=[s...]
    pallas_call x1, Pallas kernels: 3.81 us -> 2.71 us  [attend(): pl.pallas_call(finish_kernel, out_shape=jax.ShapeDtypeStruct(queries.shap...]
where the time goes in v4:
time: 43.9 us; the launch traced here: 43.7 us
  Pallas kernels  43.7 us (100%)
    pallas_call x1, Pallas kernels, attend(): pl.pallas_call(functools.partial(kernel, n), out_shape=state, in_specs=[s...  41 us
    pallas_call x1, Pallas kernels, attend(): pl.pallas_call(finish_kernel, out_shape=jax.ShapeDtypeStruct(queries.shap...  2.71 us

profile of v4, /device:TPU:1, one launch (start us, length us, event | category | flops | bytes accessed | tf_op | source)
XLA Modules:
  0.0 43.7 jit_solution(7388245421689178694)
XLA Ops:
  0.0 41.0 %shard_map.73 = (bf16[2,2048,256]{2,1,0:T(8,128)(2,1)S(1)}, f32[2,2048,256]{2,1,0:T(8,128)S(1)}, f32[2,2048,128]{2,1,0:T(8,128)S(1)}, bf16[2,2,1024,128]{3,2,1,0:T(8,128)(2,1)S(1)}) custom-call(s32[32]{0:T(128)} %slot_ref.1, s32[2]{0:T(128)} %len_ref.3, bf16[2,2048,128]{2,1,0:T(8,128)(2,1)} %bitcast.6, bf16[2,256,128]{2,1,0:T(8,128)(2,1)} %bitcast.9, ...), custom_call_target="tpu_custom_call" | custom-call | tf_op jit(solution)/shard_map/pallas_call | solution.py:322
  41.0 2.7 %shard_map.74 = bf16[2,2048,128]{2,1,0:T(8,128)(2,1)} custom-call(s32[2]{0:T(128)} %len_ref.3, bf16[2,2048,256]{2,1,0:T(8,128)(2,1)S(1)} %get-tuple-element.9.qx, f32[2,2048,256]{2,1,0:T(8,128)S(1)} %get-tuple-element.10.acc, f32[2,2048,128]{2,1,0:T(8,128)S(1)} %get-tuple-element.11.top, bf16[2,2,1024,128]{3,2,1,0:T(8,128)(2,1)S(1)} %get-tuple-element.12.kvb), custom_call_target="tpu_custom_call" | custom-call | tf_op jit(solution)/shard_map/pallas_call | solution.py:338

commit v5 on v4

--- a/solution.py
+++ b/solution.py
@@ -13,7 +13,7 @@
 F32 = jnp.float32
 
 
-CHUNKS = (4, 2, 2)
+CHUNKS = (4, 4)
 
 
 def scores_of(query, keys):
@@ -271,31 +271,38 @@
     start = kvb.shape[2] - kx.shape[1]
     tile = 512
     bufs = (s0, s1)
+    step = kx.shape[1] // 2
+
+    def put(j, at, number, total):
+        ov[j, at, :] = (number / total).astype(ov.dtype)
+        pltpu.make_async_copy(ov.at[j, at], out_ref.at[j, at], sem).start()
+
+    def divide(j):
+        for t in range(rows // tile):
+            at = pl.ds(t * tile, tile)
+            put(j, at, acc[j, at, :dim], acc[j, at, dim:])
+
+    def attend_to(size, j):
+        keys, values = kx.at[:, pl.ds(0, size)], vx.at[:, pl.ds(0, size)]
+
+        def scores(t):
+            bufs[t % 2][:, :size] = scores_of(qx[j, pl.ds(t * tile, tile), :], keys[j])
+
+        mark(start, j, len_ref, values)
+        prepare(start, j, kvb, keys, values)
+        scores(0)
+        for t in range(rows // tile):
+            if t + 1 < rows // tile:
+                scores(t + 1)
+            at = pl.ds(t * tile, tile)
+            _, fade, mixed = join(bufs[t % 2][:, :size], top[j, at, :], values[j])
+            put(j, at, acc[j, at, :dim] * fade + mixed[:, :dim], acc[j, at, dim:] * fade + mixed[:, dim:])
+
     for j in range(reqs):
-        def scores(t, j=j):
-            bufs[t % 2][...] = scores_of(qx[j, pl.ds(t * tile, tile), :], kx[j])
-
-        def put(at, number, total, j=j):
-            ov[j, at, :] = (number / total).astype(ov.dtype)
-            pltpu.make_async_copy(ov.at[j, at], out_ref.at[j, at], sem).start()
-
-        @pl.when(len_ref[j] > start)
-        def _(j=j, scores=scores, put=put):
-            mark(start, j, len_ref, vx)
-            prepare(start, j, kvb, kx, vx)
-            scores(0)
-            for t in range(rows // tile):
-                if t + 1 < rows // tile:
-                    scores(t + 1)
-                at = pl.ds(t * tile, tile)
-                _, fade, mixed = join(bufs[t % 2][...], top[j, at, :], vx[j])
-                put(at, acc[j, at, :dim] * fade + mixed[:, :dim], acc[j, at, dim:] * fade + mixed[:, dim:])
-
-        @pl.when(len_ref[j] <= start)
-        def _(j=j, put=put):
-            for t in range(rows // tile):
-                at = pl.ds(t * tile, tile)
-                put(at, acc[j, at, :dim], acc[j, at, dim:])
+        length = len_ref[j]
+        pl.when(length <= start)(functools.partial(divide, j))
+        pl.when((length > start) & (length <= start + step))(functools.partial(attend_to, step, j))
+        pl.when(length > start + step)(functools.partial(attend_to, 2 * step, j))
 
     pltpu.make_async_copy(ov, out_ref, sem).wait()
 

time: 43.9 us -> 41.6 us (0.948)
  Pallas kernels: 43.7 us -> 41.6 us
    pallas_call x1, Pallas kernels: 41 us -> 38 us  [attend(): pl.pallas_call(functools.partial(kernel, n), out_shape=state, in_specs=[s...]
    pallas_call x1, Pallas kernels: 2.71 us -> 3.63 us  [attend(): pl.pallas_call(finish_kernel, out_shape=jax.ShapeDtypeStruct(queries.shap...]
where the time goes in v5:
time: 41.6 us; the launch traced here: 41.8 us
  Pallas kernels  41.6 us (100%)
    pallas_call x1, Pallas kernels, attend(): pl.pallas_call(functools.partial(kernel, n), out_shape=state, in_specs=[s...  38 us
    pallas_call x1, Pallas kernels, attend(): pl.pallas_call(finish_kernel, out_shape=jax.ShapeDtypeStruct(queries.shap...  3.63 us

profile of v5, /device:TPU:1, one launch (start us, length us, event | category | flops | bytes accessed | tf_op | source)
XLA Modules:
  0.0 41.8 jit_solution(15706389491989070608)
XLA Ops:
  0.0 38.0 %shard_map.73 = (bf16[2,2048,256]{2,1,0:T(8,128)(2,1)S(1)}, f32[2,2048,256]{2,1,0:T(8,128)S(1)}, f32[2,2048,128]{2,1,0:T(8,128)S(1)}, bf16[2,2,1024,128]{3,2,1,0:T(8,128)(2,1)S(1)}) custom-call(s32[32]{0:T(128)} %slot_ref.1, s32[2]{0:T(128)} %len_ref.3, bf16[2,2048,128]{2,1,0:T(8,128)(2,1)} %bitcast.6, bf16[2,256,128]{2,1,0:T(8,128)(2,1)} %bitcast.9, ...), custom_call_target="tpu_custom_call" | custom-call | tf_op jit(solution)/shard_map/pallas_call | solution.py:329
  38.0 3.6 %shard_map.74 = bf16[2,2048,128]{2,1,0:T(8,128)(2,1)} custom-call(s32[2]{0:T(128)} %len_ref.3, bf16[2,2048,256]{2,1,0:T(8,128)(2,1)S(1)} %get-tuple-element.9.qx, f32[2,2048,256]{2,1,0:T(8,128)S(1)} %get-tuple-element.10.acc, f32[2,2048,128]{2,1,0:T(8,128)S(1)} %get-tuple-element.11.top, bf16[2,2,1024,128]{3,2,1,0:T(8,128)(2,1)S(1)} %get-tuple-element.12.kvb), custom_call_target="tpu_custom_call" | custom-call | tf_op jit(solution)/shard_map/pallas_call | solution.py:345
